TPU v7x, 256 devices: a whole 4x4x8 slice. The times are simulated.
256 devices in a mesh: wide: 32 (over y_lo, z, core), narrow: 8 (over y_hi, x).
Axes of the slice: x: 4, y: 4 (y_hi: 2, y_lo: 2; y = y_hi * 2 + y_lo), z: 8, core: 2. Of those that a mesh axis runs over, the one named last changes fastest.
Arguments:
- vectors: bfloat16 [65536, 768], P(('wide', 'narrow')), may hold values from -15 to 15
- block_sides: int32 [512], P(('wide', 'narrow')), may hold values from 0 to 1, as said below
- centers: bfloat16 [32768, 768], P(('wide', 'narrow')), may hold values from -8.5 to 8.5
Outputs:
- new_centers: bfloat16 [32768, 768], P(('wide', 'narrow'))
Inputs may be any that keep to these rules, and one draw needn't show every extreme that they name: `block_sides`: of the 2 labels of one device (consecutive runs of 2 entries), exactly half are 1.
All inputs are finite; a program needn't handle non-finite values.
Results may differ from a plain program's by a relative error of at most 0.0018.
The roundings to bfloat16 on the way count: a program that leaves them out, or rounds other values in their place, can miss the bound.
Values may be sent and summed in bfloat16 or wider, within the bound.
A program may use at most 64 MiB of HBM per device.

v0:
```python
import math
import jax
import jax.numpy as jnp
from jax import lax
from jax.sharding import PartitionSpec as P

LEVEL = 1
ITERS = 2


def from_partner(value, axis, distance):
    mask = 2**distance
    pairs = [(source, source ^ mask) for source in range(lax.axis_size(axis))]
    return lax.ppermute(value, axis, pairs)


def shifted(value, axis, steps):
    count = lax.axis_size(axis)
    pairs = [(source, (source + steps) % count) for source in range(count)]
    return lax.ppermute(value, axis, pairs)


def combined_all(part, axis, combine):
    gathered = jax.tree.map(lambda a: lax.all_gather(a, axis), part)

    def take(source):
        return jax.tree.map(lambda a: lax.dynamic_index_in_dim(a, source, 0, False), gathered)

    return lax.fori_loop(
        1, lax.axis_size(axis), lambda source, state: combine(state, take(source)), take(0)
    )


def combine_stats(first, second):
    upper = jnp.maximum(first[0], second[0])
    return (upper, first[1] * jnp.exp(first[0] - upper) + second[1] * jnp.exp(second[0] - upper))


def local(vectors, block_sides, centers):
    step_size = 2 ** (LEVEL + 1)
    cycle_len = lax.axis_size("wide") // step_size
    wide_place = lax.axis_index("wide")
    cycle_place = wide_place // step_size
    own_side = wide_place // 2**LEVEL % 2
    feat_width = vectors.shape[1]
    block_count = block_sides.shape[0]
    half_blocks = block_count // 2
    blocks = vectors.reshape(block_count, -1, feat_width)
    block_order = jnp.argsort(
        jnp.where(block_sides == own_side, 0, 1).astype(jnp.int32), stable=True
    )
    arranged = jnp.take(blocks, block_order, axis=0)
    incoming = from_partner(arranged[half_blocks:], "wide", LEVEL)
    local_rows = jnp.concatenate([arranged[:half_blocks], incoming], axis=0).reshape(-1, feat_width)
    gathered = lax.all_gather(local_rows, "narrow", axis=0, tiled=True)
    row_count = gathered.shape[0]
    shard_rows = centers.shape[0]
    score_scale = 4.0 / math.sqrt(feat_width)
    zero_index = jnp.zeros((), jnp.int32)

    def score_block(center):
        sq_norms = jnp.sum(center.astype(jnp.float32) ** 2, axis=1)
        products = lax.dot_general(
            gathered, center, (((1,), (1,)), ((), ())), preferred_element_type=jnp.float32
        )
        return score_scale * (products - 0.5 * sq_norms[None, :])

    def put_block(table, center, source):
        column = source % cycle_len * shard_rows
        return lax.dynamic_update_slice(table, score_block(center), (zero_index, column))

    def block_terms(weights, source, offset, length):
        column = source % cycle_len * shard_rows + offset
        columns = lax.dynamic_slice_in_dim(weights, column, length, 1)
        numerator = lax.dot_general(
            columns, gathered, (((0,), (0,)), ((), ())), preferred_element_type=jnp.float32
        )
        return (numerator, jnp.sum(columns.astype(jnp.float32), axis=0))

    for sweep_num in range(ITERS):
        scores = jnp.zeros((row_count, cycle_len * shard_rows), jnp.float32)
        scores = put_block(scores, centers, cycle_place)

        def stream_one(step_num, loop_state):
            current, table = loop_state
            current = shifted(current, "wide", step_size)
            return (current, put_block(table, current, cycle_place - step_num))

        current, scores = lax.fori_loop(1, cycle_len, stream_one, (centers, scores))
        row_top = jnp.max(scores, axis=1)
        row_sum = jnp.sum(jnp.exp(scores - row_top[:, None]), axis=1)
        full_top, full_sum = combined_all((row_top, row_sum), "narrow", combine_stats)
        weights = (jnp.exp(scores - full_top[:, None]) / full_sum[:, None]).astype(jnp.bfloat16)

        def gather_one(step_num, loop_state):
            moved = shifted((loop_state[0], loop_state[1]), "wide", step_size)
            added = block_terms(weights, cycle_place - step_num - 1, 0, shard_rows)
            return (moved[0] + added[0], moved[1] + added[1])

        numerator, denominator = lax.fori_loop(
            1, cycle_len, gather_one, block_terms(weights, cycle_place - 1, 0, shard_rows)
        )
        centers = ((numerator + centers.astype(jnp.float32)) / (denominator + 1.0)[:, None]).astype(
            jnp.bfloat16
        )
    return centers


def solution(mesh):
    in_specs = (P(("wide", "narrow"), None), P(("wide", "narrow")), P(("wide", "narrow"), None))
    out_specs = P(("wide", "narrow"), None)
    return jax.shard_map(local, mesh=mesh, in_specs=in_specs, out_specs=out_specs, check_vma=False)
```

profile of v0, /device:TPU:32, one launch (start us, length us, event | category | flops | bytes accessed | tf_op | source)
XLA Modules:
  0.0 849.5 jit_solution(4124487896540554424)
XLA Ops:
  18.0 68.8 %all-gather.6.cloned.1.call-done = bf16[2048,768]{1,0:T(8,128)(2,1)} async-done(((bf16[256,768]{1,0:T(8,128)(2,1)}), bf16[2048,768]{1,0:T(8,128)(2,1)}) %all-gather.6.cloned.1.call-update) | async-done | bytes 3145744 | tf_op jit(solution)/shard_map/all_gather | solution.py:55
  92.8 114.8 %while.102 = (s32[]{:T(128)}, bf16[128,768]{1,0:T(8,128)(2,1)}, f32[2048,1024]{1,0:T(8,128)}, bf16[2048,768]{1,0:T(8,128)(2,1)S(1)}, s32[]{:T(128)}, /*index=5*/...) while((s32[]{:T(128)}, bf16[128,768]{1,0:T(8,128)(2,1)}, ...), condition=%wide.region_4.5_spmd, body=%wide.region_2.4_spmd.sunk | while | flops 403472416 | bytes 5769536 | solution.py:89
  95.4 10.8 %collective-permute-done = bf16[128,768]{1,0:T(8,128)(2,1)} collective-permute-done((bf16[128,768]{1,0:T(8,128)(2,1)}, bf16[128,768]{1,0:T(8,128)(2,1)}, u32[]{:S(2)}, u32[]{:S(2)}) %collective-permute-start) | collective-permute-done | bytes 196640 | tf_op jit(solution)/shard_map/while/body/eval_jaxpr/ppermute | solution.py:20
  112.4 12.0 %collective-permute-done = bf16[128,768]{1,0:T(8,128)(2,1)} collective-permute-done((bf16[128,768]{1,0:T(8,128)(2,1)}, bf16[128,768]{1,0:T(8,128)(2,1)}, u32[]{:S(2)}, u32[]{:S(2)}) %collective-permute-start) | collective-permute-done | bytes 196640 | tf_op jit(solution)/shard_map/while/body/eval_jaxpr/ppermute | solution.py:20
  130.0 12.0 %collective-permute-done = bf16[128,768]{1,0:T(8,128)(2,1)} collective-permute-done((bf16[128,768]{1,0:T(8,128)(2,1)}, bf16[128,768]{1,0:T(8,128)(2,1)}, u32[]{:S(2)}, u32[]{:S(2)}) %collective-permute-start) | collective-permute-done | bytes 196640 | tf_op jit(solution)/shard_map/while/body/eval_jaxpr/ppermute | solution.py:20
  147.6 9.2 %collective-permute-done = bf16[128,768]{1,0:T(8,128)(2,1)} collective-permute-done((bf16[128,768]{1,0:T(8,128)(2,1)}, bf16[128,768]{1,0:T(8,128)(2,1)}, u32[]{:S(2)}, u32[]{:S(2)}) %collective-permute-start) | collective-permute-done | bytes 196640 | tf_op jit(solution)/shard_map/while/body/eval_jaxpr/ppermute | solution.py:20
  162.4 9.1 %collective-permute-done = bf16[128,768]{1,0:T(8,128)(2,1)} collective-permute-done((bf16[128,768]{1,0:T(8,128)(2,1)}, bf16[128,768]{1,0:T(8,128)(2,1)}, u32[]{:S(2)}, u32[]{:S(2)}) %collective-permute-start) | collective-permute-done | bytes 196640 | tf_op jit(solution)/shard_map/while/body/eval_jaxpr/ppermute | solution.py:20
  177.2 10.0 %collective-permute-done = bf16[128,768]{1,0:T(8,128)(2,1)} collective-permute-done((bf16[128,768]{1,0:T(8,128)(2,1)}, bf16[128,768]{1,0:T(8,128)(2,1)}, u32[]{:S(2)}, u32[]{:S(2)}) %collective-permute-start) | collective-permute-done | bytes 196640 | tf_op jit(solution)/shard_map/while/body/eval_jaxpr/ppermute | solution.py:20
  192.8 9.2 %collective-permute-done = bf16[128,768]{1,0:T(8,128)(2,1)} collective-permute-done((bf16[128,768]{1,0:T(8,128)(2,1)}, bf16[128,768]{1,0:T(8,128)(2,1)}, u32[]{:S(2)}, u32[]{:S(2)}) %collective-permute-start) | collective-permute-done | bytes 196640 | tf_op jit(solution)/shard_map/while/body/eval_jaxpr/ppermute | solution.py:20
  215.8 36.2 %all-gather.1 = f32[16384]{0:T(1024)} all-gather(f32[2048]{0:T(1024)S(1)} %exponential_reduce_fusion.1), channel_id=3, replica_groups=mesh['wide'=32,'narrow'=8] {'narrow'}, dimensions={0}, use_global_device_ids=true | all-gather | bytes 73728 | tf_op jit(solution)/shard_map/all_gather | solution.py:24
  254.2 36.3 %all-gather = f32[16384]{0:T(1024)} all-gather(f32[2048]{0:T(1024)S(1)} %reduce_max.18), channel_id=2, replica_groups=mesh['wide'=32,'narrow'=8] {'narrow'}, dimensions={0}, use_global_device_ids=true | all-gather | bytes 73728 | tf_op jit(solution)/shard_map/all_gather | solution.py:24
  305.5 155.7 %while.104 = (s32[]{:T(128)}, f32[128,768]{1,0:T(8,128)}, f32[128]{0:T(128)S(1)}, s32[]{:T(128)}, bf16[2048,1024]{1,0:T(8,128)(2,1)}, /*index=5*/bf16[2048,768]{...) while((s32[]{:T(128)}, f32[128,768]{1,0:T(8,128)}, ...), condition=%wide.region_12.13_spmd, body=%wide.region_10.12_spmd.sunk | while | flops 403275808 | bytes 6558088 | solution.py:100
  313.0 12.6 %collective-permute-done.2 = f32[128]{0:T(128)S(1)} collective-permute-done((f32[128]{0:T(128)S(1)}, f32[128]{0:T(128)S(1)}, u32[]{:S(2)}, u32[]{:S(2)}) %collective-permute-start.2) | collective-permute-done | bytes 544 | tf_op jit(solution)/shard_map/while/body/eval_jaxpr/ppermute | solution.py:20
  339.3 9.2 %collective-permute-done.2 = f32[128]{0:T(128)S(1)} collective-permute-done((f32[128]{0:T(128)S(1)}, f32[128]{0:T(128)S(1)}, u32[]{:S(2)}, u32[]{:S(2)}) %collective-permute-start.2) | collective-permute-done | bytes 544 | tf_op jit(solution)/shard_map/while/body/eval_jaxpr/ppermute | solution.py:20
  364.2 8.9 %collective-permute-done.2 = f32[128]{0:T(128)S(1)} collective-permute-done((f32[128]{0:T(128)S(1)}, f32[128]{0:T(128)S(1)}, u32[]{:S(2)}, u32[]{:S(2)}) %collective-permute-start.2) | collective-permute-done | bytes 544 | tf_op jit(solution)/shard_map/while/body/eval_jaxpr/ppermute | solution.py:20
  385.8 7.8 collective-permute-done.2
  404.2 12.3 %collective-permute-done.2 = f32[128]{0:T(128)S(1)} collective-permute-done((f32[128]{0:T(128)S(1)}, f32[128]{0:T(128)S(1)}, u32[]{:S(2)}, u32[]{:S(2)}) %collective-permute-start.2) | collective-permute-done | bytes 544 | tf_op jit(solution)/shard_map/while/body/eval_jaxpr/ppermute | solution.py:20
  425.5 13.0 %collective-permute-done.2 = f32[128]{0:T(128)S(1)} collective-permute-done((f32[128]{0:T(128)S(1)}, f32[128]{0:T(128)S(1)}, u32[]{:S(2)}, u32[]{:S(2)}) %collective-permute-start.2) | collective-permute-done | bytes 544 | tf_op jit(solution)/shard_map/while/body/eval_jaxpr/ppermute | solution.py:20
  468.4 115.8 %while.105 = (s32[]{:T(128)}, bf16[128,768]{1,0:T(8,128)(2,1)}, f32[2048,1024]{1,0:T(8,128)}, bf16[2048,768]{1,0:T(8,128)(2,1)S(1)}, s32[]{:T(128)}, /*index=5*/...) while((s32[]{:T(128)}, bf16[128,768]{1,0:T(8,128)(2,1)}, ...), condition=%wide.region_16.17_spmd, body=%wide.region_14.16_spmd.sunk | while | flops 403472416 | bytes 5769536 | solution.py:89
  472.7 7.4 collective-permute-done.3
  530.4 7.6 collective-permute-start.3
  564.1 9.0 %collective-permute-start.3 = (bf16[128,768]{1,0:T(8,128)(2,1)}, bf16[128,768]{1,0:T(8,128)(2,1)}, u32[]{:S(2)}, u32[]{:S(2)}) collective-permute-start(bf16[128,768]{1,0:T(8,128)(2,1)} %get-tuple-element.1261), channel_id=1, source_target_pairs={{0,32},{8,40},{16,48},{24,56},{32,64},{40,72},{48,80},{56,88},{64,... | collective-permute-start | bytes 589832 | tf_op jit(solution)/shard_map/while/body/eval_jaxpr/ppermute | solution.py:20
  592.5 46.8 %all-gather.3 = f32[16384]{0:T(1024)} all-gather(f32[2048]{0:T(1024)S(1)} %exponential_reduce_fusion), channel_id=5, replica_groups=mesh['wide'=32,'narrow'=8] {'narrow'}, dimensions={0}, use_global_device_ids=true | all-gather | bytes 73728 | tf_op jit(solution)/shard_map/all_gather | solution.py:24
  641.5 36.4 %all-gather.2 = f32[16384]{0:T(1024)} all-gather(f32[2048]{0:T(1024)S(1)} %reduce_max.19), channel_id=4, replica_groups=mesh['wide'=32,'narrow'=8] {'narrow'}, dimensions={0}, use_global_device_ids=true | all-gather | bytes 73728 | tf_op jit(solution)/shard_map/all_gather | solution.py:24
  692.9 147.9 %while.107 = (s32[]{:T(128)}, f32[128,768]{1,0:T(8,128)}, f32[128]{0:T(128)S(1)}, s32[]{:T(128)}, bf16[2048,1024]{1,0:T(8,128)(2,1)}, /*index=5*/bf16[2048,768]{...) while((s32[]{:T(128)}, f32[128,768]{1,0:T(8,128)}, ...), condition=%wide.region_24.25_spmd, body=%wide.region_22.24_spmd.sunk | while | flops 403275808 | bytes 6558088 | solution.py:100
  702.8 13.7 %collective-permute-done.5 = f32[128]{0:T(128)S(1)} collective-permute-done((f32[128]{0:T(128)S(1)}, f32[128]{0:T(128)S(1)}, u32[]{:S(2)}, u32[]{:S(2)}) %collective-permute-start.5) | collective-permute-done | bytes 544 | tf_op jit(solution)/shard_map/while/body/eval_jaxpr/ppermute | solution.py:20
  720.4 19.4 %collective-permute-done.5 = f32[128]{0:T(128)S(1)} collective-permute-done((f32[128]{0:T(128)S(1)}, f32[128]{0:T(128)S(1)}, u32[]{:S(2)}, u32[]{:S(2)}) %collective-permute-start.5) | collective-permute-done | bytes 544 | tf_op jit(solution)/shard_map/while/body/eval_jaxpr/ppermute | solution.py:20
  743.7 21.9 %collective-permute-done.5 = f32[128]{0:T(128)S(1)} collective-permute-done((f32[128]{0:T(128)S(1)}, f32[128]{0:T(128)S(1)}, u32[]{:S(2)}, u32[]{:S(2)}) %collective-permute-start.5) | collective-permute-done | bytes 544 | tf_op jit(solution)/shard_map/while/body/eval_jaxpr/ppermute | solution.py:20
  769.6 18.2 %collective-permute-done.5 = f32[128]{0:T(128)S(1)} collective-permute-done((f32[128]{0:T(128)S(1)}, f32[128]{0:T(128)S(1)}, u32[]{:S(2)}, u32[]{:S(2)}) %collective-permute-start.5) | collective-permute-done | bytes 544 | tf_op jit(solution)/shard_map/while/body/eval_jaxpr/ppermute | solution.py:20
  791.7 11.0 %collective-permute-done.5 = f32[128]{0:T(128)S(1)} collective-permute-done((f32[128]{0:T(128)S(1)}, f32[128]{0:T(128)S(1)}, u32[]{:S(2)}, u32[]{:S(2)}) %collective-permute-start.5) | collective-permute-done | bytes 544 | tf_op jit(solution)/shard_map/while/body/eval_jaxpr/ppermute | solution.py:20
  806.5 14.0 %collective-permute-done.5 = f32[128]{0:T(128)S(1)} collective-permute-done((f32[128]{0:T(128)S(1)}, f32[128]{0:T(128)S(1)}, u32[]{:S(2)}, u32[]{:S(2)}) %collective-permute-start.5) | collective-permute-done | bytes 544 | tf_op jit(solution)/shard_map/while/body/eval_jaxpr/ppermute | solution.py:20
  824.3 13.9 %collective-permute-done.5 = f32[128]{0:T(128)S(1)} collective-permute-done((f32[128]{0:T(128)S(1)}, f32[128]{0:T(128)S(1)}, u32[]{:S(2)}, u32[]{:S(2)}) %collective-permute-start.5) | collective-permute-done | bytes 544 | tf_op jit(solution)/shard_map/while/body/eval_jaxpr/ppermute | solution.py:20
  (252 shorter events, 351.9 us)
Async XLA Ops:
  6.5 80.2 %all-gather.6.cloned.1.call-start = ((), (), s32[]{:S(2)}) async-start(), calls=%async_computation | async-start | bytes 3538944 | tf_op jit(solution)/shard_map/all_gather | solution.py:55
  92.8 13.4 %collective-permute-start = (bf16[128,768]{1,0:T(8,128)(2,1)}, bf16[128,768]{1,0:T(8,128)(2,1)}, u32[]{:S(2)}, u32[]{:S(2)}) collective-permute-start(bf16[128,768]{1,0:T(8,128)(2,1)} %get-tuple-element.1165), channel_id=1, source_target_pairs={{0,32},{8,40},{16,48},{24,56},{32,64},{40,72},{48,80},{56,88},{64,... | collective-permute-start | bytes 589832 | tf_op jit(solution)/shard_map/while/body/eval_jaxpr/ppermute | solution.py:20
  111.8 12.6 %collective-permute-start = (bf16[128,768]{1,0:T(8,128)(2,1)}, bf16[128,768]{1,0:T(8,128)(2,1)}, u32[]{:S(2)}, u32[]{:S(2)}) collective-permute-start(bf16[128,768]{1,0:T(8,128)(2,1)} %get-tuple-element.1165), channel_id=1, source_target_pairs={{0,32},{8,40},{16,48},{24,56},{32,64},{40,72},{48,80},{56,88},{64,... | collective-permute-start | bytes 589832 | tf_op jit(solution)/shard_map/while/body/eval_jaxpr/ppermute | solution.py:20
  305.5 20.1 %collective-permute-start.1 = (f32[128,768]{1,0:T(8,128)}, f32[128,768]{1,0:T(8,128)}, u32[]{:S(2)}, u32[]{:S(2)}) collective-permute-start(f32[128,768]{1,0:T(8,128)} %get-tuple-element.1224), channel_id=1, source_target_pairs={{0,32},{8,40},{16,48},{24,56},{32,64},{40,72},{48,80},{56,88},{64,... | collective-permute-start | bytes 1179656 | tf_op jit(solution)/shard_map/while/body/eval_jaxpr/ppermute | solution.py:20
  307.0 18.6 %collective-permute-start.2 = (f32[128]{0:T(128)S(1)}, f32[128]{0:T(128)S(1)}, u32[]{:S(2)}, u32[]{:S(2)}) collective-permute-start(f32[128]{0:T(128)S(1)} %get-tuple-element.1225), channel_id=1, source_target_pairs={{0,32},{8,40},{16,48},{24,56},{32,64},{40,72},{48,80},{56,88},{64,... | collective-permute-start | bytes 1544 | tf_op jit(solution)/shard_map/while/body/eval_jaxpr/ppermute | solution.py:20
  328.1 20.3 %collective-permute-start.1 = (f32[128,768]{1,0:T(8,128)}, f32[128,768]{1,0:T(8,128)}, u32[]{:S(2)}, u32[]{:S(2)}) collective-permute-start(f32[128,768]{1,0:T(8,128)} %get-tuple-element.1224), channel_id=1, source_target_pairs={{0,32},{8,40},{16,48},{24,56},{32,64},{40,72},{48,80},{56,88},{64,... | collective-permute-start | bytes 1179656 | tf_op jit(solution)/shard_map/while/body/eval_jaxpr/ppermute | solution.py:20
  330.7 17.8 %collective-permute-start.2 = (f32[128]{0:T(128)S(1)}, f32[128]{0:T(128)S(1)}, u32[]{:S(2)}, u32[]{:S(2)}) collective-permute-start(f32[128]{0:T(128)S(1)} %get-tuple-element.1225), channel_id=1, source_target_pairs={{0,32},{8,40},{16,48},{24,56},{32,64},{40,72},{48,80},{56,88},{64,... | collective-permute-start | bytes 1544 | tf_op jit(solution)/shard_map/while/body/eval_jaxpr/ppermute | solution.py:20
  351.0 22.1 %collective-permute-start.1 = (f32[128,768]{1,0:T(8,128)}, f32[128,768]{1,0:T(8,128)}, u32[]{:S(2)}, u32[]{:S(2)}) collective-permute-start(f32[128,768]{1,0:T(8,128)} %get-tuple-element.1224), channel_id=1, source_target_pairs={{0,32},{8,40},{16,48},{24,56},{32,64},{40,72},{48,80},{56,88},{64,... | collective-permute-start | bytes 1179656 | tf_op jit(solution)/shard_map/while/body/eval_jaxpr/ppermute | solution.py:20
  358.3 14.8 %collective-permute-start.2 = (f32[128]{0:T(128)S(1)}, f32[128]{0:T(128)S(1)}, u32[]{:S(2)}, u32[]{:S(2)}) collective-permute-start(f32[128]{0:T(128)S(1)} %get-tuple-element.1225), channel_id=1, source_target_pairs={{0,32},{8,40},{16,48},{24,56},{32,64},{40,72},{48,80},{56,88},{64,... | collective-permute-start | bytes 1544 | tf_op jit(solution)/shard_map/while/body/eval_jaxpr/ppermute | solution.py:20
  375.6 18.0 %collective-permute-start.1 = (f32[128,768]{1,0:T(8,128)}, f32[128,768]{1,0:T(8,128)}, u32[]{:S(2)}, u32[]{:S(2)}) collective-permute-start(f32[128,768]{1,0:T(8,128)} %get-tuple-element.1224), channel_id=1, source_target_pairs={{0,32},{8,40},{16,48},{24,56},{32,64},{40,72},{48,80},{56,88},{64,... | collective-permute-start | bytes 1179656 | tf_op jit(solution)/shard_map/while/body/eval_jaxpr/ppermute | solution.py:20
  380.0 13.7 %collective-permute-start.2 = (f32[128]{0:T(128)S(1)}, f32[128]{0:T(128)S(1)}, u32[]{:S(2)}, u32[]{:S(2)}) collective-permute-start(f32[128]{0:T(128)S(1)} %get-tuple-element.1225), channel_id=1, source_target_pairs={{0,32},{8,40},{16,48},{24,56},{32,64},{40,72},{48,80},{56,88},{64,... | collective-permute-start | bytes 1544 | tf_op jit(solution)/shard_map/while/body/eval_jaxpr/ppermute | solution.py:20
  396.2 20.4 %collective-permute-start.1 = (f32[128,768]{1,0:T(8,128)}, f32[128,768]{1,0:T(8,128)}, u32[]{:S(2)}, u32[]{:S(2)}) collective-permute-start(f32[128,768]{1,0:T(8,128)} %get-tuple-element.1224), channel_id=1, source_target_pairs={{0,32},{8,40},{16,48},{24,56},{32,64},{40,72},{48,80},{56,88},{64,... | collective-permute-start | bytes 1179656 | tf_op jit(solution)/shard_map/while/body/eval_jaxpr/ppermute | solution.py:20
  399.6 16.9 %collective-permute-start.2 = (f32[128]{0:T(128)S(1)}, f32[128]{0:T(128)S(1)}, u32[]{:S(2)}, u32[]{:S(2)}) collective-permute-start(f32[128]{0:T(128)S(1)} %get-tuple-element.1225), channel_id=1, source_target_pairs={{0,32},{8,40},{16,48},{24,56},{32,64},{40,72},{48,80},{56,88},{64,... | collective-permute-start | bytes 1544 | tf_op jit(solution)/shard_map/while/body/eval_jaxpr/ppermute | solution.py:20
  419.1 19.5 %collective-permute-start.1 = (f32[128,768]{1,0:T(8,128)}, f32[128,768]{1,0:T(8,128)}, u32[]{:S(2)}, u32[]{:S(2)}) collective-permute-start(f32[128,768]{1,0:T(8,128)} %get-tuple-element.1224), channel_id=1, source_target_pairs={{0,32},{8,40},{16,48},{24,56},{32,64},{40,72},{48,80},{56,88},{64,... | collective-permute-start | bytes 1179656 | tf_op jit(solution)/shard_map/while/body/eval_jaxpr/ppermute | solution.py:20
  422.4 16.1 %collective-permute-start.2 = (f32[128]{0:T(128)S(1)}, f32[128]{0:T(128)S(1)}, u32[]{:S(2)}, u32[]{:S(2)}) collective-permute-start(f32[128]{0:T(128)S(1)} %get-tuple-element.1225), channel_id=1, source_target_pairs={{0,32},{8,40},{16,48},{24,56},{32,64},{40,72},{48,80},{56,88},{64,... | collective-permute-start | bytes 1544 | tf_op jit(solution)/shard_map/while/body/eval_jaxpr/ppermute | solution.py:20
  441.1 17.5 %collective-permute-start.1 = (f32[128,768]{1,0:T(8,128)}, f32[128,768]{1,0:T(8,128)}, u32[]{:S(2)}, u32[]{:S(2)}) collective-permute-start(f32[128,768]{1,0:T(8,128)} %get-tuple-element.1224), channel_id=1, source_target_pairs={{0,32},{8,40},{16,48},{24,56},{32,64},{40,72},{48,80},{56,88},{64,... | collective-permute-start | bytes 1179656 | tf_op jit(solution)/shard_map/while/body/eval_jaxpr/ppermute | solution.py:20
  444.5 14.1 %collective-permute-start.2 = (f32[128]{0:T(128)S(1)}, f32[128]{0:T(128)S(1)}, u32[]{:S(2)}, u32[]{:S(2)}) collective-permute-start(f32[128]{0:T(128)S(1)} %get-tuple-element.1225), channel_id=1, source_target_pairs={{0,32},{8,40},{16,48},{24,56},{32,64},{40,72},{48,80},{56,88},{64,... | collective-permute-start | bytes 1544 | tf_op jit(solution)/shard_map/while/body/eval_jaxpr/ppermute | solution.py:20
  530.4 13.1 %collective-permute-start.3 = (bf16[128,768]{1,0:T(8,128)(2,1)}, bf16[128,768]{1,0:T(8,128)(2,1)}, u32[]{:S(2)}, u32[]{:S(2)}) collective-permute-start(bf16[128,768]{1,0:T(8,128)(2,1)} %get-tuple-element.1261), channel_id=1, source_target_pairs={{0,32},{8,40},{16,48},{24,56},{32,64},{40,72},{48,80},{56,88},{64,... | collective-permute-start | bytes 589832 | tf_op jit(solution)/shard_map/while/body/eval_jaxpr/ppermute | solution.py:20
  564.1 14.5 %collective-permute-start.3 = (bf16[128,768]{1,0:T(8,128)(2,1)}, bf16[128,768]{1,0:T(8,128)(2,1)}, u32[]{:S(2)}, u32[]{:S(2)}) collective-permute-start(bf16[128,768]{1,0:T(8,128)(2,1)} %get-tuple-element.1261), channel_id=1, source_target_pairs={{0,32},{8,40},{16,48},{24,56},{32,64},{40,72},{48,80},{56,88},{64,... | collective-permute-start | bytes 589832 | tf_op jit(solution)/shard_map/while/body/eval_jaxpr/ppermute | solution.py:20
  692.9 23.7 %collective-permute-start.4 = (f32[128,768]{1,0:T(8,128)}, f32[128,768]{1,0:T(8,128)}, u32[]{:S(2)}, u32[]{:S(2)}) collective-permute-start(f32[128,768]{1,0:T(8,128)} %get-tuple-element.1320), channel_id=1, source_target_pairs={{0,32},{8,40},{16,48},{24,56},{32,64},{40,72},{48,80},{56,88},{64,... | collective-permute-start | bytes 1179656 | tf_op jit(solution)/shard_map/while/body/eval_jaxpr/ppermute | solution.py:20
  696.9 19.6 %collective-permute-start.5 = (f32[128]{0:T(128)S(1)}, f32[128]{0:T(128)S(1)}, u32[]{:S(2)}, u32[]{:S(2)}) collective-permute-start(f32[128]{0:T(128)S(1)} %get-tuple-element.1321), channel_id=1, source_target_pairs={{0,32},{8,40},{16,48},{24,56},{32,64},{40,72},{48,80},{56,88},{64,... | collective-permute-start | bytes 1544 | tf_op jit(solution)/shard_map/while/body/eval_jaxpr/ppermute | solution.py:20
  719.1 20.8 %collective-permute-start.4 = (f32[128,768]{1,0:T(8,128)}, f32[128,768]{1,0:T(8,128)}, u32[]{:S(2)}, u32[]{:S(2)}) collective-permute-start(f32[128,768]{1,0:T(8,128)} %get-tuple-element.1320), channel_id=1, source_target_pairs={{0,32},{8,40},{16,48},{24,56},{32,64},{40,72},{48,80},{56,88},{64,... | collective-permute-start | bytes 1179656 | tf_op jit(solution)/shard_map/while/body/eval_jaxpr/ppermute | solution.py:20
  719.1 20.8 %collective-permute-start.5 = (f32[128]{0:T(128)S(1)}, f32[128]{0:T(128)S(1)}, u32[]{:S(2)}, u32[]{:S(2)}) collective-permute-start(f32[128]{0:T(128)S(1)} %get-tuple-element.1321), channel_id=1, source_target_pairs={{0,32},{8,40},{16,48},{24,56},{32,64},{40,72},{48,80},{56,88},{64,... | collective-permute-start | bytes 1544 | tf_op jit(solution)/shard_map/while/body/eval_jaxpr/ppermute | solution.py:20
  742.4 23.3 %collective-permute-start.4 = (f32[128,768]{1,0:T(8,128)}, f32[128,768]{1,0:T(8,128)}, u32[]{:S(2)}, u32[]{:S(2)}) collective-permute-start(f32[128,768]{1,0:T(8,128)} %get-tuple-element.1320), channel_id=1, source_target_pairs={{0,32},{8,40},{16,48},{24,56},{32,64},{40,72},{48,80},{56,88},{64,... | collective-permute-start | bytes 1179656 | tf_op jit(solution)/shard_map/while/body/eval_jaxpr/ppermute | solution.py:20
  742.4 23.3 %collective-permute-start.5 = (f32[128]{0:T(128)S(1)}, f32[128]{0:T(128)S(1)}, u32[]{:S(2)}, u32[]{:S(2)}) collective-permute-start(f32[128]{0:T(128)S(1)} %get-tuple-element.1321), channel_id=1, source_target_pairs={{0,32},{8,40},{16,48},{24,56},{32,64},{40,72},{48,80},{56,88},{64,... | collective-permute-start | bytes 1544 | tf_op jit(solution)/shard_map/while/body/eval_jaxpr/ppermute | solution.py:20
  768.2 19.6 %collective-permute-start.4 = (f32[128,768]{1,0:T(8,128)}, f32[128,768]{1,0:T(8,128)}, u32[]{:S(2)}, u32[]{:S(2)}) collective-permute-start(f32[128,768]{1,0:T(8,128)} %get-tuple-element.1320), channel_id=1, source_target_pairs={{0,32},{8,40},{16,48},{24,56},{32,64},{40,72},{48,80},{56,88},{64,... | collective-permute-start | bytes 1179656 | tf_op jit(solution)/shard_map/while/body/eval_jaxpr/ppermute | solution.py:20
  768.2 19.5 %collective-permute-start.5 = (f32[128]{0:T(128)S(1)}, f32[128]{0:T(128)S(1)}, u32[]{:S(2)}, u32[]{:S(2)}) collective-permute-start(f32[128]{0:T(128)S(1)} %get-tuple-element.1321), channel_id=1, source_target_pairs={{0,32},{8,40},{16,48},{24,56},{32,64},{40,72},{48,80},{56,88},{64,... | collective-permute-start | bytes 1544 | tf_op jit(solution)/shard_map/while/body/eval_jaxpr/ppermute | solution.py:20
  790.3 12.3 %collective-permute-start.4 = (f32[128,768]{1,0:T(8,128)}, f32[128,768]{1,0:T(8,128)}, u32[]{:S(2)}, u32[]{:S(2)}) collective-permute-start(f32[128,768]{1,0:T(8,128)} %get-tuple-element.1320), channel_id=1, source_target_pairs={{0,32},{8,40},{16,48},{24,56},{32,64},{40,72},{48,80},{56,88},{64,... | collective-permute-start | bytes 1179656 | tf_op jit(solution)/shard_map/while/body/eval_jaxpr/ppermute | solution.py:20
  805.2 15.3 %collective-permute-start.4 = (f32[128,768]{1,0:T(8,128)}, f32[128,768]{1,0:T(8,128)}, u32[]{:S(2)}, u32[]{:S(2)}) collective-permute-start(f32[128,768]{1,0:T(8,128)} %get-tuple-element.1320), channel_id=1, source_target_pairs={{0,32},{8,40},{16,48},{24,56},{32,64},{40,72},{48,80},{56,88},{64,... | collective-permute-start | bytes 1179656 | tf_op jit(solution)/shard_map/while/body/eval_jaxpr/ppermute | solution.py:20
  805.2 15.3 %collective-permute-start.5 = (f32[128]{0:T(128)S(1)}, f32[128]{0:T(128)S(1)}, u32[]{:S(2)}, u32[]{:S(2)}) collective-permute-start(f32[128]{0:T(128)S(1)} %get-tuple-element.1321), channel_id=1, source_target_pairs={{0,32},{8,40},{16,48},{24,56},{32,64},{40,72},{48,80},{56,88},{64,... | collective-permute-start | bytes 1544 | tf_op jit(solution)/shard_map/while/body/eval_jaxpr/ppermute | solution.py:20
  823.0 15.2 %collective-permute-start.4 = (f32[128,768]{1,0:T(8,128)}, f32[128,768]{1,0:T(8,128)}, u32[]{:S(2)}, u32[]{:S(2)}) collective-permute-start(f32[128,768]{1,0:T(8,128)} %get-tuple-element.1320), channel_id=1, source_target_pairs={{0,32},{8,40},{16,48},{24,56},{32,64},{40,72},{48,80},{56,88},{64,... | collective-permute-start | bytes 1179656 | tf_op jit(solution)/shard_map/while/body/eval_jaxpr/ppermute | solution.py:20
  823.0 15.2 %collective-permute-start.5 = (f32[128]{0:T(128)S(1)}, f32[128]{0:T(128)S(1)}, u32[]{:S(2)}, u32[]{:S(2)}) collective-permute-start(f32[128]{0:T(128)S(1)} %get-tuple-element.1321), channel_id=1, source_target_pairs={{0,32},{8,40},{16,48},{24,56},{32,64},{40,72},{48,80},{56,88},{64,... | collective-permute-start | bytes 1544 | tf_op jit(solution)/shard_map/while/body/eval_jaxpr/ppermute | solution.py:20
  (21 other events, 146.3 us)
Sparse Core Ops, SparseCore 0:
  16.3 70.3 all-gather.5
where the time goes:
time: 853 us; the launch traced here: 849 us
  waiting for transfers between devices  368 us (43%)
  blocking collectives  156 us (18%)
  starting transfers between devices  109 us (13%)
  matrix products  82.4 us (10%)
  other arithmetic  64.4 us (8%)
  local copies, waits for them, and re-layouts  56.2 us (7%)
  between operations  13.6 us (2%)
    ppermute x42, waiting for transfers between devices, shifted(): return lax.ppermute(value, axis, pairs)  294 us
    all_gather x4, blocking collectives, combined_all(): gathered = jax.tree.map(lambda a: lax.all_gather(a, axis), part)  156 us
    ppermute x42, starting transfers between devices, shifted(): return lax.ppermute(value, axis, pairs)  107 us
    all_gather x1, waiting for transfers between devices, local(): gathered = lax.all_gather(local_rows, 'narrow', axis=0, tiled=True)  68.8 us
    dot_general x16, matrix products, score_block(): lax.dot_general(gathered, center, (((1,), (1,)), ((), ())), preferred_ele...  43.2 us
    dot_general x16, matrix products, block_terms(): lax.dot_general(columns, gathered, (((0,), (0,)), ((), ())), preferred_el...  39.2 us
    while x14, local copies, waits for them, and re-layouts  22.6 us
    reduce_sum x16, other arithmetic, block_terms(): return (numerator, jnp.sum(columns.astype(jnp.float32), axis=0))  19.1 us
  transfers between devices with their start and end apart: 44, of which 30 were waited for; matrix products, arithmetic and copies ran while one was open for 2% of the time, Pallas kernels for 0%

commit v1 on v0

--- a/solution.py
+++ b/solution.py
@@ -52,7 +52,8 @@
     arranged = jnp.take(blocks, block_order, axis=0)
     incoming = from_partner(arranged[half_blocks:], "wide", LEVEL)
     local_rows = jnp.concatenate([arranged[:half_blocks], incoming], axis=0).reshape(-1, feat_width)
-    gathered = lax.all_gather(local_rows, "narrow", axis=0, tiled=True)
+    sent = jnp.stack([local_rows] * lax.axis_size("narrow"))
+    gathered = jnp.concatenate(lax.all_to_all(sent, "narrow", 0, 0), axis=0)
     row_count = gathered.shape[0]
     shard_rows = centers.shape[0]
     score_scale = 4.0 / math.sqrt(feat_width)

time: 853 us -> 817 us (0.958); the launches traced: 849 us -> 802 us
  waiting for transfers between devices: 368 us -> 323 us
  starting transfers between devices: 109 us -> 124 us
  between operations: 13.6 us -> 0.19 us
    all_gather x1 -> x0, waiting for transfers between devices: 68.8 us -> none  [local(): gathered = lax.all_gather(local_rows, 'narrow', axis=0, tiled=True)]
    all_to_all x0 -> x1, waiting for transfers between devices: none -> 36.2 us  [local(): gathered = jnp.concatenate(lax.all_to_all(sent, 'narrow', 0, 0), axis=0)]
    ppermute x42, waiting for transfers between devices: 294 us -> 282 us  [shifted(): return lax.ppermute(value, axis, pairs)]
  transfers between devices with their start and end apart: 44 -> 44, of which waited for: 30 -> 30; matrix products, arithmetic and copies ran while one was open for 2% -> 3% of each run, Pallas kernels for 0% -> 0%
where the time goes in v1:
time: 817 us; the launch traced here: 802 us
  waiting for transfers between devices  323 us (40%)
  blocking collectives  151 us (18%)
  starting transfers between devices  124 us (15%)
  matrix products  82.4 us (10%)
  other arithmetic  64.6 us (8%)
  local copies, waits for them, and re-layouts  57.2 us (7%)
    ppermute x42, waiting for transfers between devices, shifted(): return lax.ppermute(value, axis, pairs)  282 us
    all_gather x4, blocking collectives, combined_all(): gathered = jax.tree.map(lambda a: lax.all_gather(a, axis), part)  151 us
    ppermute x42, starting transfers between devices, shifted(): return lax.ppermute(value, axis, pairs)  115 us
    dot_general x16, matrix products, score_block(): lax.dot_general(gathered, center, (((1,), (1,)), ((), ())), preferred_ele...  43.2 us
    dot_general x16, matrix products, block_terms(): lax.dot_general(columns, gathered, (((0,), (0,)), ((), ())), preferred_el...  39.2 us
    all_to_all x1, waiting for transfers between devices, local(): gathered = jnp.concatenate(lax.all_to_all(sent, 'narrow', 0, 0), axis=0)  36.2 us
    while x14, local copies, waits for them, and re-layouts  22.6 us
    reduce_sum x16, other arithmetic, block_terms(): return (numerator, jnp.sum(columns.astype(jnp.float32), axis=0))  19.1 us
  transfers between devices with their start and end apart: 44, of which 30 were waited for; matrix products, arithmetic and copies ran while one was open for 3% of the time, Pallas kernels for 0%

profile of v1, /device:TPU:32, one launch (start us, length us, event | category | flops | bytes accessed | tf_op | source)
XLA Modules:
  0.0 802.4 jit_solution(13486877700042134253)
XLA Ops:
  20.3 36.2 %all-to-all-done = bf16[8,256,768]{2,1,0:T(8,128)(2,1)S(1)} async-done(((bf16[8,256,768]{2,1,0:T(8,128)(2,1)}), bf16[8,256,768]{2,1,0:T(8,128)(2,1)S(1)}, u32[]{:S(2)}, u32[]{:S(2)}) %all-to-all-start) | async-done | bytes 3145760 | tf_op jit(solution)/shard_map/all_to_all | solution.py:56
  61.8 124.9 %while.102 = (s32[]{:T(128)}, bf16[128,768]{1,0:T(8,128)(2,1)}, f32[2048,1024]{1,0:T(8,128)}, bf16[2048,768]{1,0:T(8,128)(2,1)S(1)}, s32[]{:T(128)}, /*index=5*/...) while((s32[]{:T(128)}, bf16[128,768]{1,0:T(8,128)(2,1)}, ...), condition=%wide.region_4.5_spmd, body=%wide.region_2.4_spmd.sunk | while | flops 403472416 | bytes 5769536 | solution.py:90
  65.0 11.6 %collective-permute-done = bf16[128,768]{1,0:T(8,128)(2,1)} collective-permute-done((bf16[128,768]{1,0:T(8,128)(2,1)}, bf16[128,768]{1,0:T(8,128)(2,1)}, u32[]{:S(2)}, u32[]{:S(2)}) %collective-permute-start) | collective-permute-done | bytes 196640 | tf_op jit(solution)/shard_map/while/body/eval_jaxpr/ppermute | solution.py:20
  82.6 10.6 %collective-permute-done = bf16[128,768]{1,0:T(8,128)(2,1)} collective-permute-done((bf16[128,768]{1,0:T(8,128)(2,1)}, bf16[128,768]{1,0:T(8,128)(2,1)}, u32[]{:S(2)}, u32[]{:S(2)}) %collective-permute-start) | collective-permute-done | bytes 196640 | tf_op jit(solution)/shard_map/while/body/eval_jaxpr/ppermute | solution.py:20
  100.5 10.3 %collective-permute-done = bf16[128,768]{1,0:T(8,128)(2,1)} collective-permute-done((bf16[128,768]{1,0:T(8,128)(2,1)}, bf16[128,768]{1,0:T(8,128)(2,1)}, u32[]{:S(2)}, u32[]{:S(2)}) %collective-permute-start) | collective-permute-done | bytes 196640 | tf_op jit(solution)/shard_map/while/body/eval_jaxpr/ppermute | solution.py:20
  116.6 11.4 %collective-permute-done = bf16[128,768]{1,0:T(8,128)(2,1)} collective-permute-done((bf16[128,768]{1,0:T(8,128)(2,1)}, bf16[128,768]{1,0:T(8,128)(2,1)}, u32[]{:S(2)}, u32[]{:S(2)}) %collective-permute-start) | collective-permute-done | bytes 196640 | tf_op jit(solution)/shard_map/while/body/eval_jaxpr/ppermute | solution.py:20
  134.5 10.5 %collective-permute-done = bf16[128,768]{1,0:T(8,128)(2,1)} collective-permute-done((bf16[128,768]{1,0:T(8,128)(2,1)}, bf16[128,768]{1,0:T(8,128)(2,1)}, u32[]{:S(2)}, u32[]{:S(2)}) %collective-permute-start) | collective-permute-done | bytes 196640 | tf_op jit(solution)/shard_map/while/body/eval_jaxpr/ppermute | solution.py:20
  150.7 11.5 %collective-permute-done = bf16[128,768]{1,0:T(8,128)(2,1)} collective-permute-done((bf16[128,768]{1,0:T(8,128)(2,1)}, bf16[128,768]{1,0:T(8,128)(2,1)}, u32[]{:S(2)}, u32[]{:S(2)}) %collective-permute-start) | collective-permute-done | bytes 196640 | tf_op jit(solution)/shard_map/while/body/eval_jaxpr/ppermute | solution.py:20
  167.8 13.3 %collective-permute-done = bf16[128,768]{1,0:T(8,128)(2,1)} collective-permute-done((bf16[128,768]{1,0:T(8,128)(2,1)}, bf16[128,768]{1,0:T(8,128)(2,1)}, u32[]{:S(2)}, u32[]{:S(2)}) %collective-permute-start) | collective-permute-done | bytes 196640 | tf_op jit(solution)/shard_map/while/body/eval_jaxpr/ppermute | solution.py:20
  194.9 36.2 %all-gather.1 = f32[16384]{0:T(1024)} all-gather(f32[2048]{0:T(1024)S(1)} %exponential_reduce_fusion.1), channel_id=3, replica_groups=mesh['wide'=32,'narrow'=8] {'narrow'}, dimensions={0}, use_global_device_ids=true | all-gather | bytes 73728 | tf_op jit(solution)/shard_map/all_gather | solution.py:24
  233.3 36.3 %all-gather = f32[16384]{0:T(1024)} all-gather(f32[2048]{0:T(1024)S(1)} %reduce_max.18), channel_id=2, replica_groups=mesh['wide'=32,'narrow'=8] {'narrow'}, dimensions={0}, use_global_device_ids=true | all-gather | bytes 73728 | tf_op jit(solution)/shard_map/all_gather | solution.py:24
  284.6 142.6 %while.104 = (s32[]{:T(128)}, f32[128,768]{1,0:T(8,128)}, f32[128]{0:T(128)S(1)}, s32[]{:T(128)}, bf16[2048,1024]{1,0:T(8,128)(2,1)}, /*index=5*/bf16[2048,768]{...) while((s32[]{:T(128)}, f32[128,768]{1,0:T(8,128)}, ...), condition=%wide.region_12.13_spmd, body=%wide.region_10.12_spmd.sunk | while | flops 403275808 | bytes 6558088 | solution.py:101
  286.0 16.5 %collective-permute-done.2 = f32[128]{0:T(128)S(1)} collective-permute-done((f32[128]{0:T(128)S(1)}, f32[128]{0:T(128)S(1)}, u32[]{:S(2)}, u32[]{:S(2)}) %collective-permute-start.2) | collective-permute-done | bytes 544 | tf_op jit(solution)/shard_map/while/body/eval_jaxpr/ppermute | solution.py:20
  308.5 12.3 %collective-permute-done.2 = f32[128]{0:T(128)S(1)} collective-permute-done((f32[128]{0:T(128)S(1)}, f32[128]{0:T(128)S(1)}, u32[]{:S(2)}, u32[]{:S(2)}) %collective-permute-start.2) | collective-permute-done | bytes 544 | tf_op jit(solution)/shard_map/while/body/eval_jaxpr/ppermute | solution.py:20
  329.1 11.1 %collective-permute-done.2 = f32[128]{0:T(128)S(1)} collective-permute-done((f32[128]{0:T(128)S(1)}, f32[128]{0:T(128)S(1)}, u32[]{:S(2)}, u32[]{:S(2)}) %collective-permute-start.2) | collective-permute-done | bytes 544 | tf_op jit(solution)/shard_map/while/body/eval_jaxpr/ppermute | solution.py:20
  345.5 18.9 %collective-permute-done.2 = f32[128]{0:T(128)S(1)} collective-permute-done((f32[128]{0:T(128)S(1)}, f32[128]{0:T(128)S(1)}, u32[]{:S(2)}, u32[]{:S(2)}) %collective-permute-start.2) | collective-permute-done | bytes 544 | tf_op jit(solution)/shard_map/while/body/eval_jaxpr/ppermute | solution.py:20
  375.0 13.6 %collective-permute-done.2 = f32[128]{0:T(128)S(1)} collective-permute-done((f32[128]{0:T(128)S(1)}, f32[128]{0:T(128)S(1)}, u32[]{:S(2)}, u32[]{:S(2)}) %collective-permute-start.2) | collective-permute-done | bytes 544 | tf_op jit(solution)/shard_map/while/body/eval_jaxpr/ppermute | solution.py:20
  398.4 11.7 %collective-permute-done.2 = f32[128]{0:T(128)S(1)} collective-permute-done((f32[128]{0:T(128)S(1)}, f32[128]{0:T(128)S(1)}, u32[]{:S(2)}, u32[]{:S(2)}) %collective-permute-start.2) | collective-permute-done | bytes 544 | tf_op jit(solution)/shard_map/while/body/eval_jaxpr/ppermute | solution.py:20
  415.5 9.1 %collective-permute-done.2 = f32[128]{0:T(128)S(1)} collective-permute-done((f32[128]{0:T(128)S(1)}, f32[128]{0:T(128)S(1)}, u32[]{:S(2)}, u32[]{:S(2)}) %collective-permute-start.2) | collective-permute-done | bytes 544 | tf_op jit(solution)/shard_map/while/body/eval_jaxpr/ppermute | solution.py:20
  434.5 121.3 %while.105 = (s32[]{:T(128)}, bf16[128,768]{1,0:T(8,128)(2,1)}, f32[2048,1024]{1,0:T(8,128)}, bf16[2048,768]{1,0:T(8,128)(2,1)S(1)}, s32[]{:T(128)}, /*index=5*/...) while((s32[]{:T(128)}, bf16[128,768]{1,0:T(8,128)(2,1)}, ...), condition=%wide.region_16.17_spmd, body=%wide.region_14.16_spmd.sunk | while | flops 403472416 | bytes 5769536 | solution.py:90
  436.0 12.2 %collective-permute-done.3 = bf16[128,768]{1,0:T(8,128)(2,1)} collective-permute-done((bf16[128,768]{1,0:T(8,128)(2,1)}, bf16[128,768]{1,0:T(8,128)(2,1)}, u32[]{:S(2)}, u32[]{:S(2)}) %collective-permute-start.3) | collective-permute-done | bytes 196640 | tf_op jit(solution)/shard_map/while/body/eval_jaxpr/ppermute | solution.py:20
  455.8 10.8 %collective-permute-done.3 = bf16[128,768]{1,0:T(8,128)(2,1)} collective-permute-done((bf16[128,768]{1,0:T(8,128)(2,1)}, bf16[128,768]{1,0:T(8,128)(2,1)}, u32[]{:S(2)}, u32[]{:S(2)}) %collective-permute-start.3) | collective-permute-done | bytes 196640 | tf_op jit(solution)/shard_map/while/body/eval_jaxpr/ppermute | solution.py:20
  474.6 8.7 %collective-permute-done.3 = bf16[128,768]{1,0:T(8,128)(2,1)} collective-permute-done((bf16[128,768]{1,0:T(8,128)(2,1)}, bf16[128,768]{1,0:T(8,128)(2,1)}, u32[]{:S(2)}, u32[]{:S(2)}) %collective-permute-start.3) | collective-permute-done | bytes 196640 | tf_op jit(solution)/shard_map/while/body/eval_jaxpr/ppermute | solution.py:20
  564.0 41.6 %all-gather.3 = f32[16384]{0:T(1024)} all-gather(f32[2048]{0:T(1024)S(1)} %exponential_reduce_fusion), channel_id=5, replica_groups=mesh['wide'=32,'narrow'=8] {'narrow'}, dimensions={0}, use_global_device_ids=true | all-gather | bytes 73728 | tf_op jit(solution)/shard_map/all_gather | solution.py:24
  607.8 36.5 %all-gather.2 = f32[16384]{0:T(1024)} all-gather(f32[2048]{0:T(1024)S(1)} %reduce_max.19), channel_id=4, replica_groups=mesh['wide'=32,'narrow'=8] {'narrow'}, dimensions={0}, use_global_device_ids=true | all-gather | bytes 73728 | tf_op jit(solution)/shard_map/all_gather | solution.py:24
  659.3 141.2 %while.107 = (s32[]{:T(128)}, f32[128,768]{1,0:T(8,128)}, f32[128]{0:T(128)S(1)}, s32[]{:T(128)}, bf16[2048,1024]{1,0:T(8,128)(2,1)}, /*index=5*/bf16[2048,768]{...) while((s32[]{:T(128)}, f32[128,768]{1,0:T(8,128)}, ...), condition=%wide.region_24.25_spmd, body=%wide.region_22.24_spmd.sunk | while | flops 403275808 | bytes 6558088 | solution.py:101
  677.8 10.0 %collective-permute-start.5 = (f32[128]{0:T(128)S(1)}, f32[128]{0:T(128)S(1)}, u32[]{:S(2)}, u32[]{:S(2)}) collective-permute-start(f32[128]{0:T(128)S(1)} %get-tuple-element.1321), channel_id=1, source_target_pairs={{0,32},{8,40},{16,48},{24,56},{32,64},{40,72},{48,80},{56,88},{64,... | collective-permute-start | bytes 1544 | tf_op jit(solution)/shard_map/while/body/eval_jaxpr/ppermute | solution.py:20
  689.1 10.5 %collective-permute-done.5 = f32[128]{0:T(128)S(1)} collective-permute-done((f32[128]{0:T(128)S(1)}, f32[128]{0:T(128)S(1)}, u32[]{:S(2)}, u32[]{:S(2)}) %collective-permute-start.5) | collective-permute-done | bytes 544 | tf_op jit(solution)/shard_map/while/body/eval_jaxpr/ppermute | solution.py:20
  723.0 12.6 %collective-permute-start.5 = (f32[128]{0:T(128)S(1)}, f32[128]{0:T(128)S(1)}, u32[]{:S(2)}, u32[]{:S(2)}) collective-permute-start(f32[128]{0:T(128)S(1)} %get-tuple-element.1321), channel_id=1, source_target_pairs={{0,32},{8,40},{16,48},{24,56},{32,64},{40,72},{48,80},{56,88},{64,... | collective-permute-start | bytes 1544 | tf_op jit(solution)/shard_map/while/body/eval_jaxpr/ppermute | solution.py:20
  737.0 9.5 %collective-permute-done.5 = f32[128]{0:T(128)S(1)} collective-permute-done((f32[128]{0:T(128)S(1)}, f32[128]{0:T(128)S(1)}, u32[]{:S(2)}, u32[]{:S(2)}) %collective-permute-start.5) | collective-permute-done | bytes 544 | tf_op jit(solution)/shard_map/while/body/eval_jaxpr/ppermute | solution.py:20
  774.3 10.0 %collective-permute-done.5 = f32[128]{0:T(128)S(1)} collective-permute-done((f32[128]{0:T(128)S(1)}, f32[128]{0:T(128)S(1)}, u32[]{:S(2)}, u32[]{:S(2)}) %collective-permute-start.5) | collective-permute-done | bytes 544 | tf_op jit(solution)/shard_map/while/body/eval_jaxpr/ppermute | solution.py:20
  789.2 8.8 %collective-permute-done.5 = f32[128]{0:T(128)S(1)} collective-permute-done((f32[128]{0:T(128)S(1)}, f32[128]{0:T(128)S(1)}, u32[]{:S(2)}, u32[]{:S(2)}) %collective-permute-start.5) | collective-permute-done | bytes 544 | tf_op jit(solution)/shard_map/while/body/eval_jaxpr/ppermute | solution.py:20
  (248 shorter events, 362.6 us)
Async XLA Ops:
  10.7 45.8 %all-to-all-start = ((bf16[8,256,768]{2,1,0:T(8,128)(2,1)}), bf16[8,256,768]{2,1,0:T(8,128)(2,1)S(1)}, u32[]{:S(2)}, u32[]{:S(2)}) async-start(bf16[8,256,768]{2,1,0:T(8,128)(2,1)} %stack.3), calls=%async_computation | async-start | bytes 6291456 | tf_op jit(solution)/shard_map/all_to_all | solution.py:56
  61.8 14.8 %collective-permute-start = (bf16[128,768]{1,0:T(8,128)(2,1)}, bf16[128,768]{1,0:T(8,128)(2,1)}, u32[]{:S(2)}, u32[]{:S(2)}) collective-permute-start(bf16[128,768]{1,0:T(8,128)(2,1)} %get-tuple-element.1165), channel_id=1, source_target_pairs={{0,32},{8,40},{16,48},{24,56},{32,64},{40,72},{48,80},{56,88},{64,... | collective-permute-start | bytes 589832 | tf_op jit(solution)/shard_map/while/body/eval_jaxpr/ppermute | solution.py:20
  98.8 12.0 %collective-permute-start = (bf16[128,768]{1,0:T(8,128)(2,1)}, bf16[128,768]{1,0:T(8,128)(2,1)}, u32[]{:S(2)}, u32[]{:S(2)}) collective-permute-start(bf16[128,768]{1,0:T(8,128)(2,1)} %get-tuple-element.1165), channel_id=1, source_target_pairs={{0,32},{8,40},{16,48},{24,56},{32,64},{40,72},{48,80},{56,88},{64,... | collective-permute-start | bytes 589832 | tf_op jit(solution)/shard_map/while/body/eval_jaxpr/ppermute | solution.py:20
  167.8 13.3 %collective-permute-start = (bf16[128,768]{1,0:T(8,128)(2,1)}, bf16[128,768]{1,0:T(8,128)(2,1)}, u32[]{:S(2)}, u32[]{:S(2)}) collective-permute-start(bf16[128,768]{1,0:T(8,128)(2,1)} %get-tuple-element.1165), channel_id=1, source_target_pairs={{0,32},{8,40},{16,48},{24,56},{32,64},{40,72},{48,80},{56,88},{64,... | collective-permute-start | bytes 589832 | tf_op jit(solution)/shard_map/while/body/eval_jaxpr/ppermute | solution.py:20
  284.6 17.9 %collective-permute-start.1 = (f32[128,768]{1,0:T(8,128)}, f32[128,768]{1,0:T(8,128)}, u32[]{:S(2)}, u32[]{:S(2)}) collective-permute-start(f32[128,768]{1,0:T(8,128)} %get-tuple-element.1224), channel_id=1, source_target_pairs={{0,32},{8,40},{16,48},{24,56},{32,64},{40,72},{48,80},{56,88},{64,... | collective-permute-start | bytes 1179656 | tf_op jit(solution)/shard_map/while/body/eval_jaxpr/ppermute | solution.py:20
  284.6 17.9 %collective-permute-start.2 = (f32[128]{0:T(128)S(1)}, f32[128]{0:T(128)S(1)}, u32[]{:S(2)}, u32[]{:S(2)}) collective-permute-start(f32[128]{0:T(128)S(1)} %get-tuple-element.1225), channel_id=1, source_target_pairs={{0,32},{8,40},{16,48},{24,56},{32,64},{40,72},{48,80},{56,88},{64,... | collective-permute-start | bytes 1544 | tf_op jit(solution)/shard_map/while/body/eval_jaxpr/ppermute | solution.py:20
  305.1 15.8 %collective-permute-start.1 = (f32[128,768]{1,0:T(8,128)}, f32[128,768]{1,0:T(8,128)}, u32[]{:S(2)}, u32[]{:S(2)}) collective-permute-start(f32[128,768]{1,0:T(8,128)} %get-tuple-element.1224), channel_id=1, source_target_pairs={{0,32},{8,40},{16,48},{24,56},{32,64},{40,72},{48,80},{56,88},{64,... | collective-permute-start | bytes 1179656 | tf_op jit(solution)/shard_map/while/body/eval_jaxpr/ppermute | solution.py:20
  307.2 13.7 %collective-permute-start.2 = (f32[128]{0:T(128)S(1)}, f32[128]{0:T(128)S(1)}, u32[]{:S(2)}, u32[]{:S(2)}) collective-permute-start(f32[128]{0:T(128)S(1)} %get-tuple-element.1225), channel_id=1, source_target_pairs={{0,32},{8,40},{16,48},{24,56},{32,64},{40,72},{48,80},{56,88},{64,... | collective-permute-start | bytes 1544 | tf_op jit(solution)/shard_map/while/body/eval_jaxpr/ppermute | solution.py:20
  323.4 16.8 %collective-permute-start.1 = (f32[128,768]{1,0:T(8,128)}, f32[128,768]{1,0:T(8,128)}, u32[]{:S(2)}, u32[]{:S(2)}) collective-permute-start(f32[128,768]{1,0:T(8,128)} %get-tuple-element.1224), channel_id=1, source_target_pairs={{0,32},{8,40},{16,48},{24,56},{32,64},{40,72},{48,80},{56,88},{64,... | collective-permute-start | bytes 1179656 | tf_op jit(solution)/shard_map/while/body/eval_jaxpr/ppermute | solution.py:20
  326.8 13.4 %collective-permute-start.2 = (f32[128]{0:T(128)S(1)}, f32[128]{0:T(128)S(1)}, u32[]{:S(2)}, u32[]{:S(2)}) collective-permute-start(f32[128]{0:T(128)S(1)} %get-tuple-element.1225), channel_id=1, source_target_pairs={{0,32},{8,40},{16,48},{24,56},{32,64},{40,72},{48,80},{56,88},{64,... | collective-permute-start | bytes 1544 | tf_op jit(solution)/shard_map/while/body/eval_jaxpr/ppermute | solution.py:20
  342.7 21.7 %collective-permute-start.1 = (f32[128,768]{1,0:T(8,128)}, f32[128,768]{1,0:T(8,128)}, u32[]{:S(2)}, u32[]{:S(2)}) collective-permute-start(f32[128,768]{1,0:T(8,128)} %get-tuple-element.1224), channel_id=1, source_target_pairs={{0,32},{8,40},{16,48},{24,56},{32,64},{40,72},{48,80},{56,88},{64,... | collective-permute-start | bytes 1179656 | tf_op jit(solution)/shard_map/while/body/eval_jaxpr/ppermute | solution.py:20
  342.7 21.7 %collective-permute-start.2 = (f32[128]{0:T(128)S(1)}, f32[128]{0:T(128)S(1)}, u32[]{:S(2)}, u32[]{:S(2)}) collective-permute-start(f32[128]{0:T(128)S(1)} %get-tuple-element.1225), channel_id=1, source_target_pairs={{0,32},{8,40},{16,48},{24,56},{32,64},{40,72},{48,80},{56,88},{64,... | collective-permute-start | bytes 1544 | tf_op jit(solution)/shard_map/while/body/eval_jaxpr/ppermute | solution.py:20
  367.0 21.6 %collective-permute-start.1 = (f32[128,768]{1,0:T(8,128)}, f32[128,768]{1,0:T(8,128)}, u32[]{:S(2)}, u32[]{:S(2)}) collective-permute-start(f32[128,768]{1,0:T(8,128)} %get-tuple-element.1224), channel_id=1, source_target_pairs={{0,32},{8,40},{16,48},{24,56},{32,64},{40,72},{48,80},{56,88},{64,... | collective-permute-start | bytes 1179656 | tf_op jit(solution)/shard_map/while/body/eval_jaxpr/ppermute | solution.py:20
  367.0 21.6 %collective-permute-start.2 = (f32[128]{0:T(128)S(1)}, f32[128]{0:T(128)S(1)}, u32[]{:S(2)}, u32[]{:S(2)}) collective-permute-start(f32[128]{0:T(128)S(1)} %get-tuple-element.1225), channel_id=1, source_target_pairs={{0,32},{8,40},{16,48},{24,56},{32,64},{40,72},{48,80},{56,88},{64,... | collective-permute-start | bytes 1544 | tf_op jit(solution)/shard_map/while/body/eval_jaxpr/ppermute | solution.py:20
  391.2 18.9 %collective-permute-start.1 = (f32[128,768]{1,0:T(8,128)}, f32[128,768]{1,0:T(8,128)}, u32[]{:S(2)}, u32[]{:S(2)}) collective-permute-start(f32[128,768]{1,0:T(8,128)} %get-tuple-element.1224), channel_id=1, source_target_pairs={{0,32},{8,40},{16,48},{24,56},{32,64},{40,72},{48,80},{56,88},{64,... | collective-permute-start | bytes 1179656 | tf_op jit(solution)/shard_map/while/body/eval_jaxpr/ppermute | solution.py:20
  391.2 18.9 %collective-permute-start.2 = (f32[128]{0:T(128)S(1)}, f32[128]{0:T(128)S(1)}, u32[]{:S(2)}, u32[]{:S(2)}) collective-permute-start(f32[128]{0:T(128)S(1)} %get-tuple-element.1225), channel_id=1, source_target_pairs={{0,32},{8,40},{16,48},{24,56},{32,64},{40,72},{48,80},{56,88},{64,... | collective-permute-start | bytes 1544 | tf_op jit(solution)/shard_map/while/body/eval_jaxpr/ppermute | solution.py:20
  412.6 12.0 %collective-permute-start.1 = (f32[128,768]{1,0:T(8,128)}, f32[128,768]{1,0:T(8,128)}, u32[]{:S(2)}, u32[]{:S(2)}) collective-permute-start(f32[128,768]{1,0:T(8,128)} %get-tuple-element.1224), channel_id=1, source_target_pairs={{0,32},{8,40},{16,48},{24,56},{32,64},{40,72},{48,80},{56,88},{64,... | collective-permute-start | bytes 1179656 | tf_op jit(solution)/shard_map/while/body/eval_jaxpr/ppermute | solution.py:20
  412.7 12.0 %collective-permute-start.2 = (f32[128]{0:T(128)S(1)}, f32[128]{0:T(128)S(1)}, u32[]{:S(2)}, u32[]{:S(2)}) collective-permute-start(f32[128]{0:T(128)S(1)} %get-tuple-element.1225), channel_id=1, source_target_pairs={{0,32},{8,40},{16,48},{24,56},{32,64},{40,72},{48,80},{56,88},{64,... | collective-permute-start | bytes 1544 | tf_op jit(solution)/shard_map/while/body/eval_jaxpr/ppermute | solution.py:20
  434.5 13.8 %collective-permute-start.3 = (bf16[128,768]{1,0:T(8,128)(2,1)}, bf16[128,768]{1,0:T(8,128)(2,1)}, u32[]{:S(2)}, u32[]{:S(2)}) collective-permute-start(bf16[128,768]{1,0:T(8,128)(2,1)} %get-tuple-element.1261), channel_id=1, source_target_pairs={{0,32},{8,40},{16,48},{24,56},{32,64},{40,72},{48,80},{56,88},{64,... | collective-permute-start | bytes 589832 | tf_op jit(solution)/shard_map/while/body/eval_jaxpr/ppermute | solution.py:20
  453.8 12.8 %collective-permute-start.3 = (bf16[128,768]{1,0:T(8,128)(2,1)}, bf16[128,768]{1,0:T(8,128)(2,1)}, u32[]{:S(2)}, u32[]{:S(2)}) collective-permute-start(bf16[128,768]{1,0:T(8,128)(2,1)} %get-tuple-element.1261), channel_id=1, source_target_pairs={{0,32},{8,40},{16,48},{24,56},{32,64},{40,72},{48,80},{56,88},{64,... | collective-permute-start | bytes 589832 | tf_op jit(solution)/shard_map/while/body/eval_jaxpr/ppermute | solution.py:20
  520.3 13.6 %collective-permute-start.3 = (bf16[128,768]{1,0:T(8,128)(2,1)}, bf16[128,768]{1,0:T(8,128)(2,1)}, u32[]{:S(2)}, u32[]{:S(2)}) collective-permute-start(bf16[128,768]{1,0:T(8,128)(2,1)} %get-tuple-element.1261), channel_id=1, source_target_pairs={{0,32},{8,40},{16,48},{24,56},{32,64},{40,72},{48,80},{56,88},{64,... | collective-permute-start | bytes 589832 | tf_op jit(solution)/shard_map/while/body/eval_jaxpr/ppermute | solution.py:20
  659.3 15.9 %collective-permute-start.4 = (f32[128,768]{1,0:T(8,128)}, f32[128,768]{1,0:T(8,128)}, u32[]{:S(2)}, u32[]{:S(2)}) collective-permute-start(f32[128,768]{1,0:T(8,128)} %get-tuple-element.1320), channel_id=1, source_target_pairs={{0,32},{8,40},{16,48},{24,56},{32,64},{40,72},{48,80},{56,88},{64,... | collective-permute-start | bytes 1179656 | tf_op jit(solution)/shard_map/while/body/eval_jaxpr/ppermute | solution.py:20
  659.3 15.9 %collective-permute-start.5 = (f32[128]{0:T(128)S(1)}, f32[128]{0:T(128)S(1)}, u32[]{:S(2)}, u32[]{:S(2)}) collective-permute-start(f32[128]{0:T(128)S(1)} %get-tuple-element.1321), channel_id=1, source_target_pairs={{0,32},{8,40},{16,48},{24,56},{32,64},{40,72},{48,80},{56,88},{64,... | collective-permute-start | bytes 1544 | tf_op jit(solution)/shard_map/while/body/eval_jaxpr/ppermute | solution.py:20
  677.8 21.8 %collective-permute-start.4 = (f32[128,768]{1,0:T(8,128)}, f32[128,768]{1,0:T(8,128)}, u32[]{:S(2)}, u32[]{:S(2)}) collective-permute-start(f32[128,768]{1,0:T(8,128)} %get-tuple-element.1320), channel_id=1, source_target_pairs={{0,32},{8,40},{16,48},{24,56},{32,64},{40,72},{48,80},{56,88},{64,... | collective-permute-start | bytes 1179656 | tf_op jit(solution)/shard_map/while/body/eval_jaxpr/ppermute | solution.py:20
  677.8 21.7 %collective-permute-start.5 = (f32[128]{0:T(128)S(1)}, f32[128]{0:T(128)S(1)}, u32[]{:S(2)}, u32[]{:S(2)}) collective-permute-start(f32[128]{0:T(128)S(1)} %get-tuple-element.1321), channel_id=1, source_target_pairs={{0,32},{8,40},{16,48},{24,56},{32,64},{40,72},{48,80},{56,88},{64,... | collective-permute-start | bytes 1544 | tf_op jit(solution)/shard_map/while/body/eval_jaxpr/ppermute | solution.py:20
  702.1 15.6 %collective-permute-start.4 = (f32[128,768]{1,0:T(8,128)}, f32[128,768]{1,0:T(8,128)}, u32[]{:S(2)}, u32[]{:S(2)}) collective-permute-start(f32[128,768]{1,0:T(8,128)} %get-tuple-element.1320), channel_id=1, source_target_pairs={{0,32},{8,40},{16,48},{24,56},{32,64},{40,72},{48,80},{56,88},{64,... | collective-permute-start | bytes 1179656 | tf_op jit(solution)/shard_map/while/body/eval_jaxpr/ppermute | solution.py:20
  702.1 15.6 %collective-permute-start.5 = (f32[128]{0:T(128)S(1)}, f32[128]{0:T(128)S(1)}, u32[]{:S(2)}, u32[]{:S(2)}) collective-permute-start(f32[128]{0:T(128)S(1)} %get-tuple-element.1321), channel_id=1, source_target_pairs={{0,32},{8,40},{16,48},{24,56},{32,64},{40,72},{48,80},{56,88},{64,... | collective-permute-start | bytes 1544 | tf_op jit(solution)/shard_map/while/body/eval_jaxpr/ppermute | solution.py:20
  720.3 26.2 %collective-permute-start.4 = (f32[128,768]{1,0:T(8,128)}, f32[128,768]{1,0:T(8,128)}, u32[]{:S(2)}, u32[]{:S(2)}) collective-permute-start(f32[128,768]{1,0:T(8,128)} %get-tuple-element.1320), channel_id=1, source_target_pairs={{0,32},{8,40},{16,48},{24,56},{32,64},{40,72},{48,80},{56,88},{64,... | collective-permute-start | bytes 1179656 | tf_op jit(solution)/shard_map/while/body/eval_jaxpr/ppermute | solution.py:20
  723.0 23.4 %collective-permute-start.5 = (f32[128]{0:T(128)S(1)}, f32[128]{0:T(128)S(1)}, u32[]{:S(2)}, u32[]{:S(2)}) collective-permute-start(f32[128]{0:T(128)S(1)} %get-tuple-element.1321), channel_id=1, source_target_pairs={{0,32},{8,40},{16,48},{24,56},{32,64},{40,72},{48,80},{56,88},{64,... | collective-permute-start | bytes 1544 | tf_op jit(solution)/shard_map/while/body/eval_jaxpr/ppermute | solution.py:20
  749.0 15.4 %collective-permute-start.4 = (f32[128,768]{1,0:T(8,128)}, f32[128,768]{1,0:T(8,128)}, u32[]{:S(2)}, u32[]{:S(2)}) collective-permute-start(f32[128,768]{1,0:T(8,128)} %get-tuple-element.1320), channel_id=1, source_target_pairs={{0,32},{8,40},{16,48},{24,56},{32,64},{40,72},{48,80},{56,88},{64,... | collective-permute-start | bytes 1179656 | tf_op jit(solution)/shard_map/while/body/eval_jaxpr/ppermute | solution.py:20
  767.0 17.3 %collective-permute-start.4 = (f32[128,768]{1,0:T(8,128)}, f32[128,768]{1,0:T(8,128)}, u32[]{:S(2)}, u32[]{:S(2)}) collective-permute-start(f32[128,768]{1,0:T(8,128)} %get-tuple-element.1320), channel_id=1, source_target_pairs={{0,32},{8,40},{16,48},{24,56},{32,64},{40,72},{48,80},{56,88},{64,... | collective-permute-start | bytes 1179656 | tf_op jit(solution)/shard_map/while/body/eval_jaxpr/ppermute | solution.py:20
  769.2 15.0 %collective-permute-start.5 = (f32[128]{0:T(128)S(1)}, f32[128]{0:T(128)S(1)}, u32[]{:S(2)}, u32[]{:S(2)}) collective-permute-start(f32[128]{0:T(128)S(1)} %get-tuple-element.1321), channel_id=1, source_target_pairs={{0,32},{8,40},{16,48},{24,56},{32,64},{40,72},{48,80},{56,88},{64,... | collective-permute-start | bytes 1544 | tf_op jit(solution)/shard_map/while/body/eval_jaxpr/ppermute | solution.py:20
  (19 other events, 142.5 us)
